TPU v7x, 32 devices: a whole 2x2x4 slice. The times are simulated.
32 devices in a mesh: section: 2 (over core), dp: 4 (over y, x), tensor: 4 (over z).
Axes of the slice: x: 2, y: 2, z: 4, core: 2. Of those that a mesh axis runs over, the one named last changes fastest.
Arguments:
- section_input: bfloat16 [2, 512, 4096], P('section', 'dp'), may hold values from -60 to 60
- weights: bfloat16 [2, 4096, 4096], P('section', 'tensor', 'dp'), may hold values from -0.1875 to 0.1875
- gains: float32 [2, 4096], P('section'), may hold values from 0.1 to 1.9
- proj_seeds: int32 [2, 2], P('section'), may hold values from 0 to 99999
- out_grad: bfloat16 [512, 4096], P('dp'), may hold values from -0.75 to 0.75
- query_grads: bfloat16 [2, 256, 4096], P('section', 'dp', 'tensor'), may hold values from -0.017944336 to 0.017944336
Outputs:
- projected_grads: float32 [2, 2, 4096], P('section', None, 'tensor')
- scores: float32 [2, 256], P(None, 'dp')
All inputs are finite; a program needn't handle non-finite values.
Results may differ from a plain program's by a relative error of at most 0.033.
Values may be sent and summed in bfloat16 or wider, within the bound.
A program may use at most 64 MiB of HBM per device.

v0:
```python
import math
import jax
import jax.numpy as jnp
from jax import lax
from jax.sharding import PartitionSpec as P

R = 64
SEQS = 2
MICRO = 16
eps = 1e-05


def passed_along(value, axis, steps):
    count = lax.axis_size(axis)
    first, last = (max(0, -steps), min(count, count - steps))
    return lax.ppermute(value, axis, [(source, source + steps) for source in range(first, last)])


def sign_table(seed_value, row_count):
    row_index = lax.broadcasted_iota(jnp.int32, (row_count, R), 0)
    col_index = lax.broadcasted_iota(jnp.int32, (row_count, R), 1)
    mixing = row_index * 40503 + col_index * 9973 + seed_value * 7919 + 12345
    mixing = mixing ^ mixing >> 13
    mixing = mixing * 1274126177
    mixing = mixing ^ mixing >> 16
    parity = mixing >> 10 & 1
    return (jnp.where(parity == 1, 1.0, -1.0) * (1.0 / math.sqrt(row_count))).astype(jnp.bfloat16)


def take_rows(table, row_start):
    return lax.dynamic_slice_in_dim(table, row_start, MICRO, 0)


def body(section_input, weights, gains, proj_seeds, out_grad, query_grads):
    section_count = lax.axis_size("section")
    section_index = lax.axis_index("section")
    data_count = lax.axis_size("dp")
    data_index = lax.axis_index("dp")
    split_count = lax.axis_size("tensor")
    split_index = lax.axis_index("tensor")
    tok_rows = section_input.shape[1]
    feature_width = section_input.shape[2]
    slice_width = feature_width // split_count
    blocks = tok_rows // MICRO
    turn_count = section_count + blocks - 1
    own_start = split_index * slice_width
    gain_row = gains[0]
    hidden_in = section_input[0].astype(jnp.float32)
    radius = jnp.sqrt(jnp.mean(hidden_in * hidden_in, axis=1, keepdims=True) + eps)
    normed = hidden_in / radius
    lifted = (normed * gain_row).astype(jnp.bfloat16)
    weight_rows = lax.all_gather(weights[0], "dp", axis=1, tiled=True)
    lifted_own = lax.dynamic_slice_in_dim(lifted, own_start, slice_width, 1)
    partial_value = jnp.dot(lifted_own, weight_rows, preferred_element_type=jnp.float32)
    summed = lax.psum(partial_value.astype(jnp.bfloat16), "tensor").astype(jnp.float32)
    sigmoid_z = jax.nn.sigmoid(summed)
    slopes = sigmoid_z * (1.0 + summed * (1.0 - sigmoid_z))
    proj_in = sign_table(proj_seeds[0, 0], feature_width)
    proj_out = sign_table(proj_seeds[0, 1], feature_width)
    in_features = jnp.dot(lifted, proj_in, preferred_element_type=jnp.float32).astype(jnp.bfloat16)
    chain_depth = section_count - 1 - section_index
    at_top = section_index == section_count - 1

    def block_grad(operands):
        upstream, slope_rows, feature_rows, grad_sum = operands
        grad_pre = (upstream.astype(jnp.float32) * slope_rows).astype(jnp.bfloat16)
        out_features = jnp.dot(grad_pre, proj_out, preferred_element_type=jnp.float32).astype(
            jnp.bfloat16
        )
        grad_sum = grad_sum + lax.dot_general(
            feature_rows, out_features, (((0,), (0,)), ((), ())), preferred_element_type=jnp.float32
        )
        own_grads = lax.dot_general(
            grad_pre, weight_rows, (((1,), (1,)), ((), ())), preferred_element_type=jnp.float32
        ).astype(jnp.bfloat16)
        return (own_grads, grad_sum)

    def block_skip(operands):
        return (jnp.zeros((MICRO, slice_width), jnp.bfloat16), operands[3])

    def prepare(turn_index, upstream_in):
        block_index = turn_index.astype(jnp.int32) - chain_depth
        active = jnp.logical_and(block_index >= 0, block_index < blocks)
        row_start = jnp.clip(block_index, 0, blocks - 1) * MICRO
        top_rows = take_rows(out_grad, row_start)
        upstream = jnp.where(at_top, top_rows, upstream_in)
        return (active, row_start, upstream)

    def turn(turn_index, loop_state):
        incoming, grad_sum = loop_state
        active, row_start, upstream = prepare(turn_index, incoming)
        own_grads, grad_sum = lax.cond(
            active,
            block_grad,
            block_skip,
            (upstream, take_rows(slopes, row_start), take_rows(in_features, row_start), grad_sum),
        )
        full_grads = lax.all_gather(own_grads, "tensor", axis=1, tiled=True)

        def finish(operands):
            upstream_rows, grad_rows, normed_rows, radius_rows = operands
            scaled = grad_rows.astype(jnp.float32) * gain_row
            mean_dot = jnp.mean(scaled * normed_rows, axis=1, keepdims=True)
            return (
                upstream_rows.astype(jnp.float32) + (scaled - normed_rows * mean_dot) / radius_rows
            ).astype(jnp.bfloat16)

        def vacant(operands):
            return jnp.zeros((MICRO, feature_width), jnp.bfloat16)

        outgoing = lax.cond(
            active,
            finish,
            vacant,
            (upstream, full_grads, take_rows(normed, row_start), take_rows(radius, row_start)),
        )
        received = passed_along(outgoing, "section", -1)
        return (received, grad_sum)

    start_state = (jnp.zeros((MICRO, feature_width), jnp.bfloat16), jnp.zeros((R, R), jnp.float32))
    received, grad_sum = lax.fori_loop(0, turn_count, turn, start_state)
    flattened = grad_sum.reshape(R * R)
    piece_width = R * R // split_count
    own_part = lax.dynamic_slice_in_dim(flattened, split_index * piece_width, piece_width, 0)
    seq_index = data_index // (data_count // SEQS)
    seq_mask = (lax.broadcasted_iota(jnp.int32, (SEQS, 1), 0) == seq_index).astype(jnp.float32)
    per_seq = seq_mask * own_part[None, :]
    grads_all = lax.psum(per_seq, "dp")
    queries = query_grads[0].astype(jnp.float32)
    partial_scores = jnp.dot(grads_all, queries.T, precision=lax.Precision.HIGHEST)
    scores = lax.psum(partial_scores, ("section", "tensor"))
    return (grads_all[None], scores)


def solution(mesh):
    in_specs = (
        P("section", "dp", None),
        P("section", "tensor", "dp"),
        P("section", None),
        P("section", None),
        P("dp", None),
        P("section", "dp", "tensor"),
    )
    out_specs = (P("section", None, "tensor"), P(None, "dp"))
    return jax.shard_map(body, mesh=mesh, in_specs=in_specs, out_specs=out_specs, check_vma=False)
```

profile of v0, /device:TPU:1, one launch (start us, length us, event | category | flops | bytes accessed | tf_op | source)
XLA Modules:
  0.0 457.9 jit_solution(3057841927889815034)
XLA Ops:
  11.0 88.2 %all-gather.3.cloned.1.call-done = bf16[1,1024,4096]{2,1,0:T(8,128)(2,1)} async-done(((bf16[1,1024,1024]{2,1,0:T(8,128)(2,1)}), bf16[1,1024,4096]{2,1,0:T(8,128)(2,1)}) %all-gather.3.cloned.1.call-update) | async-done | bytes 8388624 | tf_op jit(solution)/shard_map/all_gather | solution.py:52
  99.3 5.7 %convolution_convert_fusion.2 = bf16[128,4096]{1,0:T(8,128)(2,1)} fusion(bf16[128,4096]{1,0:T(8,128)(2,1)S(1)} %get-tuple-element.421, s32[]{:T(128)S(6)} %select_n.44, bf16[1,1024,4096]{2,1,0:T(8,128)(2,1)} %all-gather.3.cloned.1.call-done), kind=kOutput, calls=%fused_computation.21 | convolution fusion | flops 1074266112 | bytes 9699332 | tf_op jit(solution)/shard_map/dot_general | solution.py:54
  111.4 45.8 %all-reduce.2.cloned.1.call-done = bf16[128,4096]{1,0:T(8,128)(2,1)} async-done(((bf16[128,4096]{1,0:T(8,128)(2,1)}), bf16[128,4096]{1,0:T(8,128)(2,1)}) %all-reduce.2.cloned.1.call-update) | async-done | bytes 1048592 | tf_op jit(solution)/shard_map/psum | solution.py:55
  159.8 263.6 %while.19 = (s32[]{:T(128)}, bf16[16,4096]{1,0:T(8,128)(2,1)S(1)}, f32[64,64]{1,0:T(8,128)}, s32[]{:T(128)}, pred[]{:T(512)}, /*index=5*/bf16[128,4096]{1,0:T(8,...) while((s32[]{:T(128)}, bf16[16,4096]{1,0:T(8,128)(2,1)S(1)}, ...), condition=%wide.region_8.9_spmd.clone, body=%wide.region_2.8_spmd.clone.sunk | while | flops 147674128 | bytes 13017286 | solution.py:121
  163.2 7.4 %conditional.6 = (bf16[16,1024]{1,0:T(8,128)(2,1)S(1)}, f32[64,64]{1,0:T(8,128)}) conditional(s32[]{:T(128)} %convert_element_type.134, f32[64,64]{1,0:T(8,128)} %get-tuple-element.548, (bf16[16,4096]{1,0:T(8,128)(2,1)S(1)}, f32[128,4096]{1,0:T(8,128)S(1)}, s32[]{:T(128)}, bf16[1024,4096]{1,0:T(8,128)(2,1)}, bf16[128,64]{1,0:T(8,128)(2,1)}, ...), branch_computations={%region_3.3_spmd, %region_4.4_spmd} | conditional | flops 143152128 | bytes 10310676 | solution.py:92
  163.2 5.6 %convolution_convert_fusion = bf16[16,1024]{1,0:T(8,128)(2,1)S(1)} fusion(bf16[1024,4096]{1,0:T(8,128)(2,1)} %get-tuple-element.308, f32[128,4096]{1,0:T(8,128)S(1)} %get-tuple-element.306, s32[]{:T(128)} %get-tuple-element.307, bf16[16,4096]{1,0:T(8,128)(2,1)S(1)} %get-tuple-element.305), kind=kOutput, calls=%fused_computation.1 | convolution fusion | flops 134430720 | bytes 8814596 | tf_op jit(solution)/shard_map/while/body/eval_jaxpr/cond/branch_1_fun/dot_general | solution.py:73
  170.6 10.4 %all_gather.13 = bf16[16,4096]{1,0:T(8,128)(2,1)S(1)} all-gather(bf16[16,1024]{1,0:T(8,128)(2,1)S(1)} %get-tuple-element.519), channel_id=1, replica_groups=mesh['section'=2,'dp'=4,'tensor'=4] {'tensor'}, dimensions={1}, use_global_device_ids=true | all-gather | bytes 163840 | tf_op jit(solution)/shard_map/while/body/eval_jaxpr/all_gather | solution.py:98
  189.0 7.4 %conditional.6 = (bf16[16,1024]{1,0:T(8,128)(2,1)S(1)}, f32[64,64]{1,0:T(8,128)}) conditional(s32[]{:T(128)} %convert_element_type.134, f32[64,64]{1,0:T(8,128)} %get-tuple-element.548, (bf16[16,4096]{1,0:T(8,128)(2,1)S(1)}, f32[128,4096]{1,0:T(8,128)S(1)}, s32[]{:T(128)}, bf16[1024,4096]{1,0:T(8,128)(2,1)}, bf16[128,64]{1,0:T(8,128)(2,1)}, ...), branch_computations={%region_3.3_spmd, %region_4.4_spmd} | conditional | flops 143152128 | bytes 10310676 | solution.py:92
  189.0 5.6 %convolution_convert_fusion = bf16[16,1024]{1,0:T(8,128)(2,1)S(1)} fusion(bf16[1024,4096]{1,0:T(8,128)(2,1)} %get-tuple-element.308, f32[128,4096]{1,0:T(8,128)S(1)} %get-tuple-element.306, s32[]{:T(128)} %get-tuple-element.307, bf16[16,4096]{1,0:T(8,128)(2,1)S(1)} %get-tuple-element.305), kind=kOutput, calls=%fused_computation.1 | convolution fusion | flops 134430720 | bytes 8814596 | tf_op jit(solution)/shard_map/while/body/eval_jaxpr/cond/branch_1_fun/dot_general | solution.py:73
  196.4 10.5 %all_gather.13 = bf16[16,4096]{1,0:T(8,128)(2,1)S(1)} all-gather(bf16[16,1024]{1,0:T(8,128)(2,1)S(1)} %get-tuple-element.519), channel_id=1, replica_groups=mesh['section'=2,'dp'=4,'tensor'=4] {'tensor'}, dimensions={1}, use_global_device_ids=true | all-gather | bytes 163840 | tf_op jit(solution)/shard_map/while/body/eval_jaxpr/all_gather | solution.py:98
  218.8 7.4 %conditional.6 = (bf16[16,1024]{1,0:T(8,128)(2,1)S(1)}, f32[64,64]{1,0:T(8,128)}) conditional(s32[]{:T(128)} %convert_element_type.134, f32[64,64]{1,0:T(8,128)} %get-tuple-element.548, (bf16[16,4096]{1,0:T(8,128)(2,1)S(1)}, f32[128,4096]{1,0:T(8,128)S(1)}, s32[]{:T(128)}, bf16[1024,4096]{1,0:T(8,128)(2,1)}, bf16[128,64]{1,0:T(8,128)(2,1)}, ...), branch_computations={%region_3.3_spmd, %region_4.4_spmd} | conditional | flops 143152128 | bytes 10310676 | solution.py:92
  218.8 5.6 %convolution_convert_fusion = bf16[16,1024]{1,0:T(8,128)(2,1)S(1)} fusion(bf16[1024,4096]{1,0:T(8,128)(2,1)} %get-tuple-element.308, f32[128,4096]{1,0:T(8,128)S(1)} %get-tuple-element.306, s32[]{:T(128)} %get-tuple-element.307, bf16[16,4096]{1,0:T(8,128)(2,1)S(1)} %get-tuple-element.305), kind=kOutput, calls=%fused_computation.1 | convolution fusion | flops 134430720 | bytes 8814596 | tf_op jit(solution)/shard_map/while/body/eval_jaxpr/cond/branch_1_fun/dot_general | solution.py:73
  226.2 10.5 %all_gather.13 = bf16[16,4096]{1,0:T(8,128)(2,1)S(1)} all-gather(bf16[16,1024]{1,0:T(8,128)(2,1)S(1)} %get-tuple-element.519), channel_id=1, replica_groups=mesh['section'=2,'dp'=4,'tensor'=4] {'tensor'}, dimensions={1}, use_global_device_ids=true | all-gather | bytes 163840 | tf_op jit(solution)/shard_map/while/body/eval_jaxpr/all_gather | solution.py:98
  248.5 7.4 %conditional.6 = (bf16[16,1024]{1,0:T(8,128)(2,1)S(1)}, f32[64,64]{1,0:T(8,128)}) conditional(s32[]{:T(128)} %convert_element_type.134, f32[64,64]{1,0:T(8,128)} %get-tuple-element.548, (bf16[16,4096]{1,0:T(8,128)(2,1)S(1)}, f32[128,4096]{1,0:T(8,128)S(1)}, s32[]{:T(128)}, bf16[1024,4096]{1,0:T(8,128)(2,1)}, bf16[128,64]{1,0:T(8,128)(2,1)}, ...), branch_computations={%region_3.3_spmd, %region_4.4_spmd} | conditional | flops 143152128 | bytes 10310676 | solution.py:92
  248.5 5.6 %convolution_convert_fusion = bf16[16,1024]{1,0:T(8,128)(2,1)S(1)} fusion(bf16[1024,4096]{1,0:T(8,128)(2,1)} %get-tuple-element.308, f32[128,4096]{1,0:T(8,128)S(1)} %get-tuple-element.306, s32[]{:T(128)} %get-tuple-element.307, bf16[16,4096]{1,0:T(8,128)(2,1)S(1)} %get-tuple-element.305), kind=kOutput, calls=%fused_computation.1 | convolution fusion | flops 134430720 | bytes 8814596 | tf_op jit(solution)/shard_map/while/body/eval_jaxpr/cond/branch_1_fun/dot_general | solution.py:73
  256.0 10.5 %all_gather.13 = bf16[16,4096]{1,0:T(8,128)(2,1)S(1)} all-gather(bf16[16,1024]{1,0:T(8,128)(2,1)S(1)} %get-tuple-element.519), channel_id=1, replica_groups=mesh['section'=2,'dp'=4,'tensor'=4] {'tensor'}, dimensions={1}, use_global_device_ids=true | all-gather | bytes 163840 | tf_op jit(solution)/shard_map/while/body/eval_jaxpr/all_gather | solution.py:98
  278.2 7.4 %conditional.6 = (bf16[16,1024]{1,0:T(8,128)(2,1)S(1)}, f32[64,64]{1,0:T(8,128)}) conditional(s32[]{:T(128)} %convert_element_type.134, f32[64,64]{1,0:T(8,128)} %get-tuple-element.548, (bf16[16,4096]{1,0:T(8,128)(2,1)S(1)}, f32[128,4096]{1,0:T(8,128)S(1)}, s32[]{:T(128)}, bf16[1024,4096]{1,0:T(8,128)(2,1)}, bf16[128,64]{1,0:T(8,128)(2,1)}, ...), branch_computations={%region_3.3_spmd, %region_4.4_spmd} | conditional | flops 143152128 | bytes 10310676 | solution.py:92
  278.3 5.6 %convolution_convert_fusion = bf16[16,1024]{1,0:T(8,128)(2,1)S(1)} fusion(bf16[1024,4096]{1,0:T(8,128)(2,1)} %get-tuple-element.308, f32[128,4096]{1,0:T(8,128)S(1)} %get-tuple-element.306, s32[]{:T(128)} %get-tuple-element.307, bf16[16,4096]{1,0:T(8,128)(2,1)S(1)} %get-tuple-element.305), kind=kOutput, calls=%fused_computation.1 | convolution fusion | flops 134430720 | bytes 8814596 | tf_op jit(solution)/shard_map/while/body/eval_jaxpr/cond/branch_1_fun/dot_general | solution.py:73
  285.7 10.5 %all_gather.13 = bf16[16,4096]{1,0:T(8,128)(2,1)S(1)} all-gather(bf16[16,1024]{1,0:T(8,128)(2,1)S(1)} %get-tuple-element.519), channel_id=1, replica_groups=mesh['section'=2,'dp'=4,'tensor'=4] {'tensor'}, dimensions={1}, use_global_device_ids=true | all-gather | bytes 163840 | tf_op jit(solution)/shard_map/while/body/eval_jaxpr/all_gather | solution.py:98
  308.0 7.4 %conditional.6 = (bf16[16,1024]{1,0:T(8,128)(2,1)S(1)}, f32[64,64]{1,0:T(8,128)}) conditional(s32[]{:T(128)} %convert_element_type.134, f32[64,64]{1,0:T(8,128)} %get-tuple-element.548, (bf16[16,4096]{1,0:T(8,128)(2,1)S(1)}, f32[128,4096]{1,0:T(8,128)S(1)}, s32[]{:T(128)}, bf16[1024,4096]{1,0:T(8,128)(2,1)}, bf16[128,64]{1,0:T(8,128)(2,1)}, ...), branch_computations={%region_3.3_spmd, %region_4.4_spmd} | conditional | flops 143152128 | bytes 10310676 | solution.py:92
  308.0 5.6 %convolution_convert_fusion = bf16[16,1024]{1,0:T(8,128)(2,1)S(1)} fusion(bf16[1024,4096]{1,0:T(8,128)(2,1)} %get-tuple-element.308, f32[128,4096]{1,0:T(8,128)S(1)} %get-tuple-element.306, s32[]{:T(128)} %get-tuple-element.307, bf16[16,4096]{1,0:T(8,128)(2,1)S(1)} %get-tuple-element.305), kind=kOutput, calls=%fused_computation.1 | convolution fusion | flops 134430720 | bytes 8814596 | tf_op jit(solution)/shard_map/while/body/eval_jaxpr/cond/branch_1_fun/dot_general | solution.py:73
  315.4 10.5 %all_gather.13 = bf16[16,4096]{1,0:T(8,128)(2,1)S(1)} all-gather(bf16[16,1024]{1,0:T(8,128)(2,1)S(1)} %get-tuple-element.519), channel_id=1, replica_groups=mesh['section'=2,'dp'=4,'tensor'=4] {'tensor'}, dimensions={1}, use_global_device_ids=true | all-gather | bytes 163840 | tf_op jit(solution)/shard_map/while/body/eval_jaxpr/all_gather | solution.py:98
  337.7 7.4 %conditional.6 = (bf16[16,1024]{1,0:T(8,128)(2,1)S(1)}, f32[64,64]{1,0:T(8,128)}) conditional(s32[]{:T(128)} %convert_element_type.134, f32[64,64]{1,0:T(8,128)} %get-tuple-element.548, (bf16[16,4096]{1,0:T(8,128)(2,1)S(1)}, f32[128,4096]{1,0:T(8,128)S(1)}, s32[]{:T(128)}, bf16[1024,4096]{1,0:T(8,128)(2,1)}, bf16[128,64]{1,0:T(8,128)(2,1)}, ...), branch_computations={%region_3.3_spmd, %region_4.4_spmd} | conditional | flops 143152128 | bytes 10310676 | solution.py:92
  337.7 5.6 %convolution_convert_fusion = bf16[16,1024]{1,0:T(8,128)(2,1)S(1)} fusion(bf16[1024,4096]{1,0:T(8,128)(2,1)} %get-tuple-element.308, f32[128,4096]{1,0:T(8,128)S(1)} %get-tuple-element.306, s32[]{:T(128)} %get-tuple-element.307, bf16[16,4096]{1,0:T(8,128)(2,1)S(1)} %get-tuple-element.305), kind=kOutput, calls=%fused_computation.1 | convolution fusion | flops 134430720 | bytes 8814596 | tf_op jit(solution)/shard_map/while/body/eval_jaxpr/cond/branch_1_fun/dot_general | solution.py:73
  345.1 10.5 %all_gather.13 = bf16[16,4096]{1,0:T(8,128)(2,1)S(1)} all-gather(bf16[16,1024]{1,0:T(8,128)(2,1)S(1)} %get-tuple-element.519), channel_id=1, replica_groups=mesh['section'=2,'dp'=4,'tensor'=4] {'tensor'}, dimensions={1}, use_global_device_ids=true | all-gather | bytes 163840 | tf_op jit(solution)/shard_map/while/body/eval_jaxpr/all_gather | solution.py:98
  367.4 7.4 %conditional.6 = (bf16[16,1024]{1,0:T(8,128)(2,1)S(1)}, f32[64,64]{1,0:T(8,128)}) conditional(s32[]{:T(128)} %convert_element_type.134, f32[64,64]{1,0:T(8,128)} %get-tuple-element.548, (bf16[16,4096]{1,0:T(8,128)(2,1)S(1)}, f32[128,4096]{1,0:T(8,128)S(1)}, s32[]{:T(128)}, bf16[1024,4096]{1,0:T(8,128)(2,1)}, bf16[128,64]{1,0:T(8,128)(2,1)}, ...), branch_computations={%region_3.3_spmd, %region_4.4_spmd} | conditional | flops 143152128 | bytes 10310676 | solution.py:92
  367.4 5.6 %convolution_convert_fusion = bf16[16,1024]{1,0:T(8,128)(2,1)S(1)} fusion(bf16[1024,4096]{1,0:T(8,128)(2,1)} %get-tuple-element.308, f32[128,4096]{1,0:T(8,128)S(1)} %get-tuple-element.306, s32[]{:T(128)} %get-tuple-element.307, bf16[16,4096]{1,0:T(8,128)(2,1)S(1)} %get-tuple-element.305), kind=kOutput, calls=%fused_computation.1 | convolution fusion | flops 134430720 | bytes 8814596 | tf_op jit(solution)/shard_map/while/body/eval_jaxpr/cond/branch_1_fun/dot_general | solution.py:73
  374.9 10.5 %all_gather.13 = bf16[16,4096]{1,0:T(8,128)(2,1)S(1)} all-gather(bf16[16,1024]{1,0:T(8,128)(2,1)S(1)} %get-tuple-element.519), channel_id=1, replica_groups=mesh['section'=2,'dp'=4,'tensor'=4] {'tensor'}, dimensions={1}, use_global_device_ids=true | all-gather | bytes 163840 | tf_op jit(solution)/shard_map/while/body/eval_jaxpr/all_gather | solution.py:98
  397.2 10.5 %all_gather.13 = bf16[16,4096]{1,0:T(8,128)(2,1)S(1)} all-gather(bf16[16,1024]{1,0:T(8,128)(2,1)S(1)} %get-tuple-element.519), channel_id=1, replica_groups=mesh['section'=2,'dp'=4,'tensor'=4] {'tensor'}, dimensions={1}, use_global_device_ids=true | all-gather | bytes 163840 | tf_op jit(solution)/shard_map/while/body/eval_jaxpr/all_gather | solution.py:98
  407.7 14.8 %collective-permute-start = (bf16[16,4096]{1,0:T(8,128)(2,1)S(1)}, bf16[16,4096]{1,0:T(8,128)(2,1)S(1)}, u32[]{:S(2)}, u32[]{:S(2)}) collective-permute-start(bf16[16,4096]{1,0:T(8,128)(2,1)S(1)} %get-tuple-element.588), channel_id=1, source_target_pairs={{16,0},{17,1},{18,2},{19,3},{20,4},{21,5},{22,6},{23,7},{24,8},{25... | collective-permute-start | bytes 393224 | tf_op jit(solution)/shard_map/while/body/eval_jaxpr/ppermute | solution.py:16
  425.0 7.8 %psum.22 = f32[2,1024]{1,0:T(2,128)S(1)} all-reduce(f32[2,1024]{1,0:T(2,128)S(1)} %broadcast_multiply_fusion.1), channel_id=1, replica_groups=mesh['section'=2,'dp'=4,'tensor'=4] {'dp'}, use_global_device_ids=true, to_apply=%region_9.10 | all-reduce | flops 2048 | bytes 16384 | tf_op jit(solution)/shard_map/psum | solution.py:128
  433.0 18.1 %psum.23 = f32[2,64]{1,0:T(2,128)} all-reduce(f32[2,64]{1,0:T(2,128)S(1)} %fusion.32), channel_id=1, replica_groups=mesh['section'=2,'dp'=4,'tensor'=4] {'section','tensor'}, use_global_device_ids=true, to_apply=%region_10.11 | all-reduce | flops 128 | bytes 1024 | tf_op jit(solution)/shard_map/psum | solution.py:131
  (135 shorter events, 140.9 us)
Async XLA Ops:
  7.2 425.6 %copy-start = (bf16[1,64,1024]{2,1,0:T(8,128)(2,1)S(1)}, bf16[1,64,1024]{2,1,0:T(8,128)(2,1)}, u32[]{:S(2)}) copy-start(bf16[1,64,1024]{2,1,0:T(8,128)(2,1)} %param.17) | copy-start | bytes 393220
  7.2 1.3 copy-start.1
  7.2 2.1 copy-start.2
  7.2 92.1 %all-gather.3.cloned.1.call-start = ((), (), s32[]{:S(2)}) async-start(), calls=%async_computation.1 | async-start | bytes 10485760 | tf_op jit(solution)/shard_map/all_gather | solution.py:52
  7.9 149.3 %all-reduce.2.cloned.1.call-start = ((), (), s32[]{:S(2)}) async-start(), calls=%async_computation | async-start | bytes 2097152 | tf_op jit(solution)/shard_map/psum | solution.py:55
  99.3 5.7 %copy-start.4 = (s32[1,2]{1,0:T(1,128)S(1)}, s32[1,2]{1,0:T(1,128)}, u32[]{:S(2)}) copy-start(s32[1,2]{1,0:T(1,128)} %param.15) | copy-start | bytes 28
  163.2 17.9 %copy-start.5 = (f32[128,1]{0,1:T(1,128)S(1)}, f32[128,1]{0,1:T(1,128)}, u32[]{:S(2)}) copy-start(f32[128,1]{0,1:T(1,128)} %get-tuple-element.578) | copy-start | bytes 1540 | tf_op jit(solution)/shard_map/while
  183.4 2.3 collective-permute-start
  189.0 17.9 %copy-start.5 = (f32[128,1]{0,1:T(1,128)S(1)}, f32[128,1]{0,1:T(1,128)}, u32[]{:S(2)}) copy-start(f32[128,1]{0,1:T(1,128)} %get-tuple-element.578) | copy-start | bytes 1540 | tf_op jit(solution)/shard_map/while
  209.3 6.2 %collective-permute-start = (bf16[16,4096]{1,0:T(8,128)(2,1)S(1)}, bf16[16,4096]{1,0:T(8,128)(2,1)S(1)}, u32[]{:S(2)}, u32[]{:S(2)}) collective-permute-start(bf16[16,4096]{1,0:T(8,128)(2,1)S(1)} %get-tuple-element.588), channel_id=1, source_target_pairs={{16,0},{17,1},{18,2},{19,3},{20,4},{21,5},{22,6},{23,7},{24,8},{25... | collective-permute-start | bytes 393224 | tf_op jit(solution)/shard_map/while/body/eval_jaxpr/ppermute | solution.py:16
  218.8 17.9 %copy-start.5 = (f32[128,1]{0,1:T(1,128)S(1)}, f32[128,1]{0,1:T(1,128)}, u32[]{:S(2)}) copy-start(f32[128,1]{0,1:T(1,128)} %get-tuple-element.578) | copy-start | bytes 1540 | tf_op jit(solution)/shard_map/while
  239.1 6.2 %collective-permute-start = (bf16[16,4096]{1,0:T(8,128)(2,1)S(1)}, bf16[16,4096]{1,0:T(8,128)(2,1)S(1)}, u32[]{:S(2)}, u32[]{:S(2)}) collective-permute-start(bf16[16,4096]{1,0:T(8,128)(2,1)S(1)} %get-tuple-element.588), channel_id=1, source_target_pairs={{16,0},{17,1},{18,2},{19,3},{20,4},{21,5},{22,6},{23,7},{24,8},{25... | collective-permute-start | bytes 393224 | tf_op jit(solution)/shard_map/while/body/eval_jaxpr/ppermute | solution.py:16
  248.5 17.9 %copy-start.5 = (f32[128,1]{0,1:T(1,128)S(1)}, f32[128,1]{0,1:T(1,128)}, u32[]{:S(2)}) copy-start(f32[128,1]{0,1:T(1,128)} %get-tuple-element.578) | copy-start | bytes 1540 | tf_op jit(solution)/shard_map/while
  268.8 6.1 %collective-permute-start = (bf16[16,4096]{1,0:T(8,128)(2,1)S(1)}, bf16[16,4096]{1,0:T(8,128)(2,1)S(1)}, u32[]{:S(2)}, u32[]{:S(2)}) collective-permute-start(bf16[16,4096]{1,0:T(8,128)(2,1)S(1)} %get-tuple-element.588), channel_id=1, source_target_pairs={{16,0},{17,1},{18,2},{19,3},{20,4},{21,5},{22,6},{23,7},{24,8},{25... | collective-permute-start | bytes 393224 | tf_op jit(solution)/shard_map/while/body/eval_jaxpr/ppermute | solution.py:16
  278.2 17.9 %copy-start.5 = (f32[128,1]{0,1:T(1,128)S(1)}, f32[128,1]{0,1:T(1,128)}, u32[]{:S(2)}) copy-start(f32[128,1]{0,1:T(1,128)} %get-tuple-element.578) | copy-start | bytes 1540 | tf_op jit(solution)/shard_map/while
  298.5 6.1 %collective-permute-start = (bf16[16,4096]{1,0:T(8,128)(2,1)S(1)}, bf16[16,4096]{1,0:T(8,128)(2,1)S(1)}, u32[]{:S(2)}, u32[]{:S(2)}) collective-permute-start(bf16[16,4096]{1,0:T(8,128)(2,1)S(1)} %get-tuple-element.588), channel_id=1, source_target_pairs={{16,0},{17,1},{18,2},{19,3},{20,4},{21,5},{22,6},{23,7},{24,8},{25... | collective-permute-start | bytes 393224 | tf_op jit(solution)/shard_map/while/body/eval_jaxpr/ppermute | solution.py:16
  308.0 17.9 %copy-start.5 = (f32[128,1]{0,1:T(1,128)S(1)}, f32[128,1]{0,1:T(1,128)}, u32[]{:S(2)}) copy-start(f32[128,1]{0,1:T(1,128)} %get-tuple-element.578) | copy-start | bytes 1540 | tf_op jit(solution)/shard_map/while
  328.3 6.1 %collective-permute-start = (bf16[16,4096]{1,0:T(8,128)(2,1)S(1)}, bf16[16,4096]{1,0:T(8,128)(2,1)S(1)}, u32[]{:S(2)}, u32[]{:S(2)}) collective-permute-start(bf16[16,4096]{1,0:T(8,128)(2,1)S(1)} %get-tuple-element.588), channel_id=1, source_target_pairs={{16,0},{17,1},{18,2},{19,3},{20,4},{21,5},{22,6},{23,7},{24,8},{25... | collective-permute-start | bytes 393224 | tf_op jit(solution)/shard_map/while/body/eval_jaxpr/ppermute | solution.py:16
  337.7 17.9 %copy-start.5 = (f32[128,1]{0,1:T(1,128)S(1)}, f32[128,1]{0,1:T(1,128)}, u32[]{:S(2)}) copy-start(f32[128,1]{0,1:T(1,128)} %get-tuple-element.578) | copy-start | bytes 1540 | tf_op jit(solution)/shard_map/while
  358.0 6.1 %collective-permute-start = (bf16[16,4096]{1,0:T(8,128)(2,1)S(1)}, bf16[16,4096]{1,0:T(8,128)(2,1)S(1)}, u32[]{:S(2)}, u32[]{:S(2)}) collective-permute-start(bf16[16,4096]{1,0:T(8,128)(2,1)S(1)} %get-tuple-element.588), channel_id=1, source_target_pairs={{16,0},{17,1},{18,2},{19,3},{20,4},{21,5},{22,6},{23,7},{24,8},{25... | collective-permute-start | bytes 393224 | tf_op jit(solution)/shard_map/while/body/eval_jaxpr/ppermute | solution.py:16
  367.4 17.9 %copy-start.5 = (f32[128,1]{0,1:T(1,128)S(1)}, f32[128,1]{0,1:T(1,128)}, u32[]{:S(2)}) copy-start(f32[128,1]{0,1:T(1,128)} %get-tuple-element.578) | copy-start | bytes 1540 | tf_op jit(solution)/shard_map/while
  387.6 6.2 %collective-permute-start = (bf16[16,4096]{1,0:T(8,128)(2,1)S(1)}, bf16[16,4096]{1,0:T(8,128)(2,1)S(1)}, u32[]{:S(2)}, u32[]{:S(2)}) collective-permute-start(bf16[16,4096]{1,0:T(8,128)(2,1)S(1)} %get-tuple-element.588), channel_id=1, source_target_pairs={{16,0},{17,1},{18,2},{19,3},{20,4},{21,5},{22,6},{23,7},{24,8},{25... | collective-permute-start | bytes 393224 | tf_op jit(solution)/shard_map/while/body/eval_jaxpr/ppermute | solution.py:16
  397.1 10.5 %copy-start.5 = (f32[128,1]{0,1:T(1,128)S(1)}, f32[128,1]{0,1:T(1,128)}, u32[]{:S(2)}) copy-start(f32[128,1]{0,1:T(1,128)} %get-tuple-element.578) | copy-start | bytes 1540 | tf_op jit(solution)/shard_map/while
  407.7 15.8 %collective-permute-start = (bf16[16,4096]{1,0:T(8,128)(2,1)S(1)}, bf16[16,4096]{1,0:T(8,128)(2,1)S(1)}, u32[]{:S(2)}, u32[]{:S(2)}) collective-permute-start(bf16[16,4096]{1,0:T(8,128)(2,1)S(1)} %get-tuple-element.588), channel_id=1, source_target_pairs={{16,0},{17,1},{18,2},{19,3},{20,4},{21,5},{22,6},{23,7},{24,8},{25... | collective-permute-start | bytes 393224 | tf_op jit(solution)/shard_map/while/body/eval_jaxpr/ppermute | solution.py:16
  432.8 18.3 %copy-start.3 = (f32[2,1024]{1,0:T(2,128)}, f32[2,1024]{1,0:T(2,128)S(1)}, u32[]{:S(2)}) copy-start(f32[2,1024]{1,0:T(2,128)S(1)} %psum.22) | copy-start | bytes 24580
Sparse Core Ops, SparseCore 0:
  9.9 89.3 all-gather.2
  105.1 52.1 all-reduce.1
where the time goes:
time: 461 us; the launch traced here: 458 us
  waiting for transfers between devices  143 us (31%)
  blocking collectives  120 us (26%)
  matrix products  67.3 us (15%)
  other arithmetic  54.6 us (12%)
  starting transfers between devices  52.6 us (11%)
  between operations  15.4 us (3%)
    all_gather x9, blocking collectives, turn(): full_grads = lax.all_gather(own_grads, 'tensor', axis=1, tiled=True)  94.2 us
    all_gather x1, waiting for transfers between devices, body(): weight_rows = lax.all_gather(weights[0], 'dp', axis=1, tiled=True)  88.2 us
    ppermute x9, starting transfers between devices, passed_along(): lax.ppermute(value, axis, [(source, source + steps) for source in range(f...  52.5 us
    psum x1, waiting for transfers between devices, body(): lax.psum(partial_value.astype(jnp.bfloat16), 'tensor').astype(jnp.float32)  45.8 us
    dot_general x8, matrix products, block_grad(): lax.dot_general(grad_pre, weight_rows, (((1,), (1,)), ((), ())), preferre...  45.2 us
    convert_element_type x9, other arithmetic, sign_table(): (jnp.where(parity == 1, 1.0, -1.0) * (1.0 / math.sqrt(row_count))).astype...  21 us
    psum x1, blocking collectives, body(): scores = lax.psum(partial_scores, ('section', 'tensor'))  18.1 us
    dot_general x8, matrix products, block_grad(): lax.dot_general(feature_rows, out_features, (((0,), (0,)), ((), ())), pre...  14.2 us
  transfers between devices with their start and end apart: 11, of which 11 were waited for; matrix products, arithmetic and copies ran while one was open for 2% of the time, Pallas kernels for 0%

commit v1 on v0

--- a/solution.py
+++ b/solution.py
@@ -3,11 +3,17 @@
 import jax.numpy as jnp
 from jax import lax
 from jax.sharding import PartitionSpec as P
+from jax.lax import all_gather
 
 R = 64
 SEQS = 2
 MICRO = 16
 eps = 1e-05
+
+
+def settle_slot_up(incoming_x):
+    low = all_gather(incoming_x, axis_name="dp")
+    return jnp.concatenate(low, axis=1)
 
 
 def passed_along(value, axis, steps):
@@ -49,7 +55,7 @@
     radius = jnp.sqrt(jnp.mean(hidden_in * hidden_in, axis=1, keepdims=True) + eps)
     normed = hidden_in / radius
     lifted = (normed * gain_row).astype(jnp.bfloat16)
-    weight_rows = lax.all_gather(weights[0], "dp", axis=1, tiled=True)
+    weight_rows = settle_slot_up(weights[0])
     lifted_own = lax.dynamic_slice_in_dim(lifted, own_start, slice_width, 1)
     partial_value = jnp.dot(lifted_own, weight_rows, preferred_element_type=jnp.float32)
     summed = lax.psum(partial_value.astype(jnp.bfloat16), "tensor").astype(jnp.float32)

time: 461 us -> 475 us (1.030)
  local copies, waits for them, and re-layouts: 3.93 us -> 26.8 us
  waiting for transfers between devices: 143 us -> 132 us
    all_gather x0 -> x1, local copies, waits for them, and re-layouts: none -> 11.4 us  [settle_slot_up(): low = all_gather(incoming_x, axis_name='dp')]
    unnamed x11 -> x12, local copies, waits for them, and re-layouts: 1.2 us -> 12.6 us
    psum x1, waiting for transfers between devices: 45.8 us -> 34.5 us  [body(): lax.psum(partial_value.astype(jnp.bfloat16), 'tensor').astype(jnp.float32)]
  transfers between devices with their start and end apart: 11 -> 11, of which waited for: 11 -> 11; matrix products, arithmetic and copies ran while one was open for 2% -> 4% of each run, Pallas kernels for 0% -> 0%
where the time goes in v1:
time: 475 us; the launch traced here: 471 us
  waiting for transfers between devices  132 us (28%)
  blocking collectives  120 us (25%)
  matrix products  69 us (15%)
  other arithmetic  54.8 us (12%)
  starting transfers between devices  52.6 us (11%)
  local copies, waits for them, and re-layouts  26.8 us (6%)
  between operations  15.4 us (3%)
    all_gather x9, blocking collectives, turn(): full_grads = lax.all_gather(own_grads, 'tensor', axis=1, tiled=True)  94.2 us
    all_gather x1, waiting for transfers between devices, settle_slot_up(): low = all_gather(incoming_x, axis_name='dp')  88.2 us
    ppermute x9, starting transfers between devices, passed_along(): lax.ppermute(value, axis, [(source, source + steps) for source in range(f...  52.5 us
    dot_general x8, matrix products, block_grad(): lax.dot_general(grad_pre, weight_rows, (((1,), (1,)), ((), ())), preferre...  45.2 us
    psum x1, waiting for transfers between devices, body(): lax.psum(partial_value.astype(jnp.bfloat16), 'tensor').astype(jnp.float32)  34.5 us
    convert_element_type x9, other arithmetic, sign_table(): (jnp.where(parity == 1, 1.0, -1.0) * (1.0 / math.sqrt(row_count))).astype...  21.1 us
    psum x1, blocking collectives, body(): scores = lax.psum(partial_scores, ('section', 'tensor'))  18.1 us
    dot_general x8, matrix products, block_grad(): lax.dot_general(feature_rows, out_features, (((0,), (0,)), ((), ())), pre...  14.2 us
  transfers between devices with their start and end apart: 11, of which 11 were waited for; matrix products, arithmetic and copies ran while one was open for 4% of the time, Pallas kernels for 0%

profile of v1, /device:TPU:1, one launch (start us, length us, event | category | flops | bytes accessed | tf_op | source)
XLA Modules:
  0.0 471.1 jit_solution(14049588950372934262)
XLA Ops:
  11.1 88.2 %all-gather.2.cloned.1.call-done = bf16[4,1024,1024]{2,1,0:T(8,128)(2,1)} async-done(((bf16[1,1024,1024]{2,1,0:T(8,128)(2,1)}), bf16[4,1024,1024]{2,1,0:T(8,128)(2,1)}) %all-gather.2.cloned.1.call-update) | async-done | bytes 8388624 | tf_op jit(solution)/shard_map/all_gather | solution.py:15
  99.3 11.4 %copy.11 = bf16[4,1024,1024]{1,2,0:T(8,128)(2,1)} copy(bf16[4,1024,1024]{2,1,0:T(8,128)(2,1)} %all-gather.2.cloned.1.call-done) | data formatting | bytes 16777216 | tf_op jit(solution)/shard_map/all_gather | solution.py:15
  110.7 7.3 %convolution_convert_fusion.2 = bf16[128,4096]{1,0:T(8,128)(2,1)} fusion(bf16[1024,4096]{0,1:T(8,128)(2,1)} %bitcast.26, bf16[128,4096]{1,0:T(8,128)(2,1)S(1)} %get-tuple-element.451, s32[]{:T(128)S(6)} %select_n.44), kind=kOutput, calls=%fused_computation.21 | convolution fusion | flops 1074266112 | bytes 9699332 | tf_op jit(solution)/shard_map/dot_general | solution.py:60
  124.4 11.4 %copy.12 = bf16[1024,4096]{1,0:T(8,128)(2,1)} copy(bf16[1024,4096]{0,1:T(8,128)(2,1)} %bitcast.27) | data formatting | bytes 16777216
  135.8 34.5 %all-reduce.2.cloned.1.call-done = bf16[128,4096]{1,0:T(8,128)(2,1)} async-done(((bf16[128,4096]{1,0:T(8,128)(2,1)}), bf16[128,4096]{1,0:T(8,128)(2,1)}) %all-reduce.2.cloned.1.call-update) | async-done | bytes 1048592 | tf_op jit(solution)/shard_map/psum | solution.py:61
  172.9 263.8 %while.19 = (s32[]{:T(128)}, bf16[16,4096]{1,0:T(8,128)(2,1)S(1)}, f32[64,64]{1,0:T(8,128)}, s32[]{:T(128)}, pred[]{:T(512)}, /*index=5*/bf16[128,4096]{1,0:T(8,...) while((s32[]{:T(128)}, bf16[16,4096]{1,0:T(8,128)(2,1)S(1)}, ...), condition=%wide.region_8.9_spmd.clone, body=%wide.region_2.8_spmd.clone.sunk | while | flops 147674128 | bytes 13017286 | solution.py:127
  176.2 7.5 %conditional.6 = (bf16[16,1024]{1,0:T(8,128)(2,1)S(1)}, f32[64,64]{1,0:T(8,128)}) conditional(s32[]{:T(128)} %convert_element_type.134, f32[64,64]{1,0:T(8,128)} %get-tuple-element.578, (bf16[16,4096]{1,0:T(8,128)(2,1)S(1)}, f32[128,4096]{1,0:T(8,128)S(1)}, s32[]{:T(128)}, bf16[1024,4096]{1,0:T(8,128)(2,1)}, bf16[128,64]{1,0:T(8,128)(2,1)}, ...), branch_computations={%region_3.3_spmd, %region_4.4_spmd} | conditional | flops 143152128 | bytes 10310676 | solution.py:98
  176.3 5.6 %convolution_convert_fusion = bf16[16,1024]{1,0:T(8,128)(2,1)S(1)} fusion(bf16[1024,4096]{1,0:T(8,128)(2,1)} %get-tuple-element.308, f32[128,4096]{1,0:T(8,128)S(1)} %get-tuple-element.306, s32[]{:T(128)} %get-tuple-element.307, bf16[16,4096]{1,0:T(8,128)(2,1)S(1)} %get-tuple-element.305), kind=kOutput, calls=%fused_computation.1 | convolution fusion | flops 134430720 | bytes 8814596 | tf_op jit(solution)/shard_map/while/body/eval_jaxpr/cond/branch_1_fun/dot_general | solution.py:79
  183.7 10.4 %all_gather.13 = bf16[16,4096]{1,0:T(8,128)(2,1)S(1)} all-gather(bf16[16,1024]{1,0:T(8,128)(2,1)S(1)} %get-tuple-element.549), channel_id=1, replica_groups=mesh['section'=2,'dp'=4,'tensor'=4] {'tensor'}, dimensions={1}, use_global_device_ids=true | all-gather | bytes 163840 | tf_op jit(solution)/shard_map/while/body/eval_jaxpr/all_gather | solution.py:104
  202.1 7.5 %conditional.6 = (bf16[16,1024]{1,0:T(8,128)(2,1)S(1)}, f32[64,64]{1,0:T(8,128)}) conditional(s32[]{:T(128)} %convert_element_type.134, f32[64,64]{1,0:T(8,128)} %get-tuple-element.578, (bf16[16,4096]{1,0:T(8,128)(2,1)S(1)}, f32[128,4096]{1,0:T(8,128)S(1)}, s32[]{:T(128)}, bf16[1024,4096]{1,0:T(8,128)(2,1)}, bf16[128,64]{1,0:T(8,128)(2,1)}, ...), branch_computations={%region_3.3_spmd, %region_4.4_spmd} | conditional | flops 143152128 | bytes 10310676 | solution.py:98
  202.1 5.6 %convolution_convert_fusion = bf16[16,1024]{1,0:T(8,128)(2,1)S(1)} fusion(bf16[1024,4096]{1,0:T(8,128)(2,1)} %get-tuple-element.308, f32[128,4096]{1,0:T(8,128)S(1)} %get-tuple-element.306, s32[]{:T(128)} %get-tuple-element.307, bf16[16,4096]{1,0:T(8,128)(2,1)S(1)} %get-tuple-element.305), kind=kOutput, calls=%fused_computation.1 | convolution fusion | flops 134430720 | bytes 8814596 | tf_op jit(solution)/shard_map/while/body/eval_jaxpr/cond/branch_1_fun/dot_general | solution.py:79
  209.5 10.5 %all_gather.13 = bf16[16,4096]{1,0:T(8,128)(2,1)S(1)} all-gather(bf16[16,1024]{1,0:T(8,128)(2,1)S(1)} %get-tuple-element.549), channel_id=1, replica_groups=mesh['section'=2,'dp'=4,'tensor'=4] {'tensor'}, dimensions={1}, use_global_device_ids=true | all-gather | bytes 163840 | tf_op jit(solution)/shard_map/while/body/eval_jaxpr/all_gather | solution.py:104
  231.9 7.5 %conditional.6 = (bf16[16,1024]{1,0:T(8,128)(2,1)S(1)}, f32[64,64]{1,0:T(8,128)}) conditional(s32[]{:T(128)} %convert_element_type.134, f32[64,64]{1,0:T(8,128)} %get-tuple-element.578, (bf16[16,4096]{1,0:T(8,128)(2,1)S(1)}, f32[128,4096]{1,0:T(8,128)S(1)}, s32[]{:T(128)}, bf16[1024,4096]{1,0:T(8,128)(2,1)}, bf16[128,64]{1,0:T(8,128)(2,1)}, ...), branch_computations={%region_3.3_spmd, %region_4.4_spmd} | conditional | flops 143152128 | bytes 10310676 | solution.py:98
  239.3 10.5 %all_gather.13 = bf16[16,4096]{1,0:T(8,128)(2,1)S(1)} all-gather(bf16[16,1024]{1,0:T(8,128)(2,1)S(1)} %get-tuple-element.549), channel_id=1, replica_groups=mesh['section'=2,'dp'=4,'tensor'=4] {'tensor'}, dimensions={1}, use_global_device_ids=true | all-gather | bytes 163840 | tf_op jit(solution)/shard_map/while/body/eval_jaxpr/all_gather | solution.py:104
  261.6 7.5 %conditional.6 = (bf16[16,1024]{1,0:T(8,128)(2,1)S(1)}, f32[64,64]{1,0:T(8,128)}) conditional(s32[]{:T(128)} %convert_element_type.134, f32[64,64]{1,0:T(8,128)} %get-tuple-element.578, (bf16[16,4096]{1,0:T(8,128)(2,1)S(1)}, f32[128,4096]{1,0:T(8,128)S(1)}, s32[]{:T(128)}, bf16[1024,4096]{1,0:T(8,128)(2,1)}, bf16[128,64]{1,0:T(8,128)(2,1)}, ...), branch_computations={%region_3.3_spmd, %region_4.4_spmd} | conditional | flops 143152128 | bytes 10310676 | solution.py:98
  261.7 5.6 %convolution_convert_fusion = bf16[16,1024]{1,0:T(8,128)(2,1)S(1)} fusion(bf16[1024,4096]{1,0:T(8,128)(2,1)} %get-tuple-element.308, f32[128,4096]{1,0:T(8,128)S(1)} %get-tuple-element.306, s32[]{:T(128)} %get-tuple-element.307, bf16[16,4096]{1,0:T(8,128)(2,1)S(1)} %get-tuple-element.305), kind=kOutput, calls=%fused_computation.1 | convolution fusion | flops 134430720 | bytes 8814596 | tf_op jit(solution)/shard_map/while/body/eval_jaxpr/cond/branch_1_fun/dot_general | solution.py:79
  269.1 10.5 %all_gather.13 = bf16[16,4096]{1,0:T(8,128)(2,1)S(1)} all-gather(bf16[16,1024]{1,0:T(8,128)(2,1)S(1)} %get-tuple-element.549), channel_id=1, replica_groups=mesh['section'=2,'dp'=4,'tensor'=4] {'tensor'}, dimensions={1}, use_global_device_ids=true | all-gather | bytes 163840 | tf_op jit(solution)/shard_map/while/body/eval_jaxpr/all_gather | solution.py:104
  291.4 7.5 %conditional.6 = (bf16[16,1024]{1,0:T(8,128)(2,1)S(1)}, f32[64,64]{1,0:T(8,128)}) conditional(s32[]{:T(128)} %convert_element_type.134, f32[64,64]{1,0:T(8,128)} %get-tuple-element.578, (bf16[16,4096]{1,0:T(8,128)(2,1)S(1)}, f32[128,4096]{1,0:T(8,128)S(1)}, s32[]{:T(128)}, bf16[1024,4096]{1,0:T(8,128)(2,1)}, bf16[128,64]{1,0:T(8,128)(2,1)}, ...), branch_computations={%region_3.3_spmd, %region_4.4_spmd} | conditional | flops 143152128 | bytes 10310676 | solution.py:98
  291.4 5.6 %convolution_convert_fusion = bf16[16,1024]{1,0:T(8,128)(2,1)S(1)} fusion(bf16[1024,4096]{1,0:T(8,128)(2,1)} %get-tuple-element.308, f32[128,4096]{1,0:T(8,128)S(1)} %get-tuple-element.306, s32[]{:T(128)} %get-tuple-element.307, bf16[16,4096]{1,0:T(8,128)(2,1)S(1)} %get-tuple-element.305), kind=kOutput, calls=%fused_computation.1 | convolution fusion | flops 134430720 | bytes 8814596 | tf_op jit(solution)/shard_map/while/body/eval_jaxpr/cond/branch_1_fun/dot_general | solution.py:79
  298.8 10.5 %all_gather.13 = bf16[16,4096]{1,0:T(8,128)(2,1)S(1)} all-gather(bf16[16,1024]{1,0:T(8,128)(2,1)S(1)} %get-tuple-element.549), channel_id=1, replica_groups=mesh['section'=2,'dp'=4,'tensor'=4] {'tensor'}, dimensions={1}, use_global_device_ids=true | all-gather | bytes 163840 | tf_op jit(solution)/shard_map/while/body/eval_jaxpr/all_gather | solution.py:104
  321.1 7.5 %conditional.6 = (bf16[16,1024]{1,0:T(8,128)(2,1)S(1)}, f32[64,64]{1,0:T(8,128)}) conditional(s32[]{:T(128)} %convert_element_type.134, f32[64,64]{1,0:T(8,128)} %get-tuple-element.578, (bf16[16,4096]{1,0:T(8,128)(2,1)S(1)}, f32[128,4096]{1,0:T(8,128)S(1)}, s32[]{:T(128)}, bf16[1024,4096]{1,0:T(8,128)(2,1)}, bf16[128,64]{1,0:T(8,128)(2,1)}, ...), branch_computations={%region_3.3_spmd, %region_4.4_spmd} | conditional | flops 143152128 | bytes 10310676 | solution.py:98
  328.6 10.5 %all_gather.13 = bf16[16,4096]{1,0:T(8,128)(2,1)S(1)} all-gather(bf16[16,1024]{1,0:T(8,128)(2,1)S(1)} %get-tuple-element.549), channel_id=1, replica_groups=mesh['section'=2,'dp'=4,'tensor'=4] {'tensor'}, dimensions={1}, use_global_device_ids=true | all-gather | bytes 163840 | tf_op jit(solution)/shard_map/while/body/eval_jaxpr/all_gather | solution.py:104
  350.9 7.5 %conditional.6 = (bf16[16,1024]{1,0:T(8,128)(2,1)S(1)}, f32[64,64]{1,0:T(8,128)}) conditional(s32[]{:T(128)} %convert_element_type.134, f32[64,64]{1,0:T(8,128)} %get-tuple-element.578, (bf16[16,4096]{1,0:T(8,128)(2,1)S(1)}, f32[128,4096]{1,0:T(8,128)S(1)}, s32[]{:T(128)}, bf16[1024,4096]{1,0:T(8,128)(2,1)}, bf16[128,64]{1,0:T(8,128)(2,1)}, ...), branch_computations={%region_3.3_spmd, %region_4.4_spmd} | conditional | flops 143152128 | bytes 10310676 | solution.py:98
  350.9 5.6 %convolution_convert_fusion = bf16[16,1024]{1,0:T(8,128)(2,1)S(1)} fusion(bf16[1024,4096]{1,0:T(8,128)(2,1)} %get-tuple-element.308, f32[128,4096]{1,0:T(8,128)S(1)} %get-tuple-element.306, s32[]{:T(128)} %get-tuple-element.307, bf16[16,4096]{1,0:T(8,128)(2,1)S(1)} %get-tuple-element.305), kind=kOutput, calls=%fused_computation.1 | convolution fusion | flops 134430720 | bytes 8814596 | tf_op jit(solution)/shard_map/while/body/eval_jaxpr/cond/branch_1_fun/dot_general | solution.py:79
  358.3 10.5 %all_gather.13 = bf16[16,4096]{1,0:T(8,128)(2,1)S(1)} all-gather(bf16[16,1024]{1,0:T(8,128)(2,1)S(1)} %get-tuple-element.549), channel_id=1, replica_groups=mesh['section'=2,'dp'=4,'tensor'=4] {'tensor'}, dimensions={1}, use_global_device_ids=true | all-gather | bytes 163840 | tf_op jit(solution)/shard_map/while/body/eval_jaxpr/all_gather | solution.py:104
  380.6 7.4 %conditional.6 = (bf16[16,1024]{1,0:T(8,128)(2,1)S(1)}, f32[64,64]{1,0:T(8,128)}) conditional(s32[]{:T(128)} %convert_element_type.134, f32[64,64]{1,0:T(8,128)} %get-tuple-element.578, (bf16[16,4096]{1,0:T(8,128)(2,1)S(1)}, f32[128,4096]{1,0:T(8,128)S(1)}, s32[]{:T(128)}, bf16[1024,4096]{1,0:T(8,128)(2,1)}, bf16[128,64]{1,0:T(8,128)(2,1)}, ...), branch_computations={%region_3.3_spmd, %region_4.4_spmd} | conditional | flops 143152128 | bytes 10310676 | solution.py:98
  380.6 5.6 %convolution_convert_fusion = bf16[16,1024]{1,0:T(8,128)(2,1)S(1)} fusion(bf16[1024,4096]{1,0:T(8,128)(2,1)} %get-tuple-element.308, f32[128,4096]{1,0:T(8,128)S(1)} %get-tuple-element.306, s32[]{:T(128)} %get-tuple-element.307, bf16[16,4096]{1,0:T(8,128)(2,1)S(1)} %get-tuple-element.305), kind=kOutput, calls=%fused_computation.1 | convolution fusion | flops 134430720 | bytes 8814596 | tf_op jit(solution)/shard_map/while/body/eval_jaxpr/cond/branch_1_fun/dot_general | solution.py:79
  388.0 10.5 %all_gather.13 = bf16[16,4096]{1,0:T(8,128)(2,1)S(1)} all-gather(bf16[16,1024]{1,0:T(8,128)(2,1)S(1)} %get-tuple-element.549), channel_id=1, replica_groups=mesh['section'=2,'dp'=4,'tensor'=4] {'tensor'}, dimensions={1}, use_global_device_ids=true | all-gather | bytes 163840 | tf_op jit(solution)/shard_map/while/body/eval_jaxpr/all_gather | solution.py:104
  410.4 10.5 %all_gather.13 = bf16[16,4096]{1,0:T(8,128)(2,1)S(1)} all-gather(bf16[16,1024]{1,0:T(8,128)(2,1)S(1)} %get-tuple-element.549), channel_id=1, replica_groups=mesh['section'=2,'dp'=4,'tensor'=4] {'tensor'}, dimensions={1}, use_global_device_ids=true | all-gather | bytes 163840 | tf_op jit(solution)/shard_map/while/body/eval_jaxpr/all_gather | solution.py:104
  420.9 14.8 %collective-permute-start = (bf16[16,4096]{1,0:T(8,128)(2,1)S(1)}, bf16[16,4096]{1,0:T(8,128)(2,1)S(1)}, u32[]{:S(2)}, u32[]{:S(2)}) collective-permute-start(bf16[16,4096]{1,0:T(8,128)(2,1)S(1)} %get-tuple-element.618), channel_id=1, source_target_pairs={{16,0},{17,1},{18,2},{19,3},{20,4},{21,5},{22,6},{23,7},{24,8},{25... | collective-permute-start | bytes 393224 | tf_op jit(solution)/shard_map/while/body/eval_jaxpr/ppermute | solution.py:22
  438.2 7.8 %psum.22 = f32[2,1024]{1,0:T(2,128)S(1)} all-reduce(f32[2,1024]{1,0:T(2,128)S(1)} %broadcast_multiply_fusion.1), channel_id=1, replica_groups=mesh['section'=2,'dp'=4,'tensor'=4] {'dp'}, use_global_device_ids=true, to_apply=%region_9.10 | all-reduce | flops 2048 | bytes 16384 | tf_op jit(solution)/shard_map/psum | solution.py:134
  446.2 18.1 %psum.23 = f32[2,64]{1,0:T(2,128)} all-reduce(f32[2,64]{1,0:T(2,128)S(1)} %fusion.32), channel_id=1, replica_groups=mesh['section'=2,'dp'=4,'tensor'=4] {'section','tensor'}, use_global_device_ids=true, to_apply=%region_10.11 | all-reduce | flops 128 | bytes 1024 | tf_op jit(solution)/shard_map/psum | solution.py:137
  (137 shorter events, 152.4 us)
Async XLA Ops:
  7.2 438.9 %copy-start = (bf16[1,64,1024]{2,1,0:T(8,128)(2,1)S(1)}, bf16[1,64,1024]{2,1,0:T(8,128)(2,1)}, u32[]{:S(2)}) copy-start(bf16[1,64,1024]{2,1,0:T(8,128)(2,1)} %param.17) | copy-start | bytes 393220
  7.2 1.3 copy-start.1
  7.2 2.1 copy-start.2
  7.2 92.1 %all-gather.2.cloned.1.call-start = ((), (), s32[]{:S(2)}) async-start(), calls=%async_computation | async-start | bytes 10485760 | tf_op jit(solution)/shard_map/all_gather | solution.py:15
  7.9 162.4 %all-reduce.2.cloned.1.call-start = ((), (), s32[]{:S(2)}) async-start(), calls=%async_computation.1 | async-start | bytes 2097152 | tf_op jit(solution)/shard_map/psum | solution.py:61
  110.7 7.3 %copy-start.4 = (s32[1,2]{1,0:T(1,128)S(1)}, s32[1,2]{1,0:T(1,128)}, u32[]{:S(2)}) copy-start(s32[1,2]{1,0:T(1,128)} %param.15) | copy-start | bytes 28
  176.2 17.9 %copy-start.5 = (f32[128,1]{0,1:T(1,128)S(1)}, f32[128,1]{0,1:T(1,128)}, u32[]{:S(2)}) copy-start(f32[128,1]{0,1:T(1,128)} %get-tuple-element.608) | copy-start | bytes 1540 | tf_op jit(solution)/shard_map/while
  196.5 2.3 collective-permute-start
  202.1 17.9 %copy-start.5 = (f32[128,1]{0,1:T(1,128)S(1)}, f32[128,1]{0,1:T(1,128)}, u32[]{:S(2)}) copy-start(f32[128,1]{0,1:T(1,128)} %get-tuple-element.608) | copy-start | bytes 1540 | tf_op jit(solution)/shard_map/while
  222.4 6.2 %collective-permute-start = (bf16[16,4096]{1,0:T(8,128)(2,1)S(1)}, bf16[16,4096]{1,0:T(8,128)(2,1)S(1)}, u32[]{:S(2)}, u32[]{:S(2)}) collective-permute-start(bf16[16,4096]{1,0:T(8,128)(2,1)S(1)} %get-tuple-element.618), channel_id=1, source_target_pairs={{16,0},{17,1},{18,2},{19,3},{20,4},{21,5},{22,6},{23,7},{24,8},{25... | collective-permute-start | bytes 393224 | tf_op jit(solution)/shard_map/while/body/eval_jaxpr/ppermute | solution.py:22
  231.9 17.9 %copy-start.5 = (f32[128,1]{0,1:T(1,128)S(1)}, f32[128,1]{0,1:T(1,128)}, u32[]{:S(2)}) copy-start(f32[128,1]{0,1:T(1,128)} %get-tuple-element.608) | copy-start | bytes 1540 | tf_op jit(solution)/shard_map/while
  252.2 6.2 %collective-permute-start = (bf16[16,4096]{1,0:T(8,128)(2,1)S(1)}, bf16[16,4096]{1,0:T(8,128)(2,1)S(1)}, u32[]{:S(2)}, u32[]{:S(2)}) collective-permute-start(bf16[16,4096]{1,0:T(8,128)(2,1)S(1)} %get-tuple-element.618), channel_id=1, source_target_pairs={{16,0},{17,1},{18,2},{19,3},{20,4},{21,5},{22,6},{23,7},{24,8},{25... | collective-permute-start | bytes 393224 | tf_op jit(solution)/shard_map/while/body/eval_jaxpr/ppermute | solution.py:22
  261.6 17.9 %copy-start.5 = (f32[128,1]{0,1:T(1,128)S(1)}, f32[128,1]{0,1:T(1,128)}, u32[]{:S(2)}) copy-start(f32[128,1]{0,1:T(1,128)} %get-tuple-element.608) | copy-start | bytes 1540 | tf_op jit(solution)/shard_map/while
  281.9 6.1 %collective-permute-start = (bf16[16,4096]{1,0:T(8,128)(2,1)S(1)}, bf16[16,4096]{1,0:T(8,128)(2,1)S(1)}, u32[]{:S(2)}, u32[]{:S(2)}) collective-permute-start(bf16[16,4096]{1,0:T(8,128)(2,1)S(1)} %get-tuple-element.618), channel_id=1, source_target_pairs={{16,0},{17,1},{18,2},{19,3},{20,4},{21,5},{22,6},{23,7},{24,8},{25... | collective-permute-start | bytes 393224 | tf_op jit(solution)/shard_map/while/body/eval_jaxpr/ppermute | solution.py:22
  291.4 17.9 %copy-start.5 = (f32[128,1]{0,1:T(1,128)S(1)}, f32[128,1]{0,1:T(1,128)}, u32[]{:S(2)}) copy-start(f32[128,1]{0,1:T(1,128)} %get-tuple-element.608) | copy-start | bytes 1540 | tf_op jit(solution)/shard_map/while
  311.7 6.1 %collective-permute-start = (bf16[16,4096]{1,0:T(8,128)(2,1)S(1)}, bf16[16,4096]{1,0:T(8,128)(2,1)S(1)}, u32[]{:S(2)}, u32[]{:S(2)}) collective-permute-start(bf16[16,4096]{1,0:T(8,128)(2,1)S(1)} %get-tuple-element.618), channel_id=1, source_target_pairs={{16,0},{17,1},{18,2},{19,3},{20,4},{21,5},{22,6},{23,7},{24,8},{25... | collective-permute-start | bytes 393224 | tf_op jit(solution)/shard_map/while/body/eval_jaxpr/ppermute | solution.py:22
  321.1 17.9 %copy-start.5 = (f32[128,1]{0,1:T(1,128)S(1)}, f32[128,1]{0,1:T(1,128)}, u32[]{:S(2)}) copy-start(f32[128,1]{0,1:T(1,128)} %get-tuple-element.608) | copy-start | bytes 1540 | tf_op jit(solution)/shard_map/while
  341.4 6.1 %collective-permute-start = (bf16[16,4096]{1,0:T(8,128)(2,1)S(1)}, bf16[16,4096]{1,0:T(8,128)(2,1)S(1)}, u32[]{:S(2)}, u32[]{:S(2)}) collective-permute-start(bf16[16,4096]{1,0:T(8,128)(2,1)S(1)} %get-tuple-element.618), channel_id=1, source_target_pairs={{16,0},{17,1},{18,2},{19,3},{20,4},{21,5},{22,6},{23,7},{24,8},{25... | collective-permute-start | bytes 393224 | tf_op jit(solution)/shard_map/while/body/eval_jaxpr/ppermute | solution.py:22
  350.9 17.9 %copy-start.5 = (f32[128,1]{0,1:T(1,128)S(1)}, f32[128,1]{0,1:T(1,128)}, u32[]{:S(2)}) copy-start(f32[128,1]{0,1:T(1,128)} %get-tuple-element.608) | copy-start | bytes 1540 | tf_op jit(solution)/shard_map/while
  371.2 6.1 %collective-permute-start = (bf16[16,4096]{1,0:T(8,128)(2,1)S(1)}, bf16[16,4096]{1,0:T(8,128)(2,1)S(1)}, u32[]{:S(2)}, u32[]{:S(2)}) collective-permute-start(bf16[16,4096]{1,0:T(8,128)(2,1)S(1)} %get-tuple-element.618), channel_id=1, source_target_pairs={{16,0},{17,1},{18,2},{19,3},{20,4},{21,5},{22,6},{23,7},{24,8},{25... | collective-permute-start | bytes 393224 | tf_op jit(solution)/shard_map/while/body/eval_jaxpr/ppermute | solution.py:22
  380.6 17.9 %copy-start.5 = (f32[128,1]{0,1:T(1,128)S(1)}, f32[128,1]{0,1:T(1,128)}, u32[]{:S(2)}) copy-start(f32[128,1]{0,1:T(1,128)} %get-tuple-element.608) | copy-start | bytes 1540 | tf_op jit(solution)/shard_map/while
  400.8 6.2 %collective-permute-start = (bf16[16,4096]{1,0:T(8,128)(2,1)S(1)}, bf16[16,4096]{1,0:T(8,128)(2,1)S(1)}, u32[]{:S(2)}, u32[]{:S(2)}) collective-permute-start(bf16[16,4096]{1,0:T(8,128)(2,1)S(1)} %get-tuple-element.618), channel_id=1, source_target_pairs={{16,0},{17,1},{18,2},{19,3},{20,4},{21,5},{22,6},{23,7},{24,8},{25... | collective-permute-start | bytes 393224 | tf_op jit(solution)/shard_map/while/body/eval_jaxpr/ppermute | solution.py:22
  410.3 10.5 %copy-start.5 = (f32[128,1]{0,1:T(1,128)S(1)}, f32[128,1]{0,1:T(1,128)}, u32[]{:S(2)}) copy-start(f32[128,1]{0,1:T(1,128)} %get-tuple-element.608) | copy-start | bytes 1540 | tf_op jit(solution)/shard_map/while
  420.9 15.8 %collective-permute-start = (bf16[16,4096]{1,0:T(8,128)(2,1)S(1)}, bf16[16,4096]{1,0:T(8,128)(2,1)S(1)}, u32[]{:S(2)}, u32[]{:S(2)}) collective-permute-start(bf16[16,4096]{1,0:T(8,128)(2,1)S(1)} %get-tuple-element.618), channel_id=1, source_target_pairs={{16,0},{17,1},{18,2},{19,3},{20,4},{21,5},{22,6},{23,7},{24,8},{25... | collective-permute-start | bytes 393224 | tf_op jit(solution)/shard_map/while/body/eval_jaxpr/ppermute | solution.py:22
  446.0 18.3 %copy-start.3 = (f32[2,1024]{1,0:T(2,128)}, f32[2,1024]{1,0:T(2,128)S(1)}, u32[]{:S(2)}) copy-start(f32[2,1024]{1,0:T(2,128)S(1)} %psum.22) | copy-start | bytes 24580
Sparse Core Ops, SparseCore 0:
  9.9 89.3 all-gather.1
  118.1 52.1 all-reduce.1
